TPU v7x, 768 devices: a whole 4x8x12 slice. The times are simulated.
768 devices in a mesh: dp: 32 (over y, x), tensor: 24 (over z, core).
Axes of the slice: x: 4, y: 8, z: 12, core: 2. Of those that a mesh axis runs over, the one named last changes fastest.
Arguments:
- kept_input: bfloat16 [18432, 4096], P(('dp', 'tensor')), may hold values from -6 to 6
- kept_grad: bfloat16 [18432, 4096], P(('dp', 'tensor')), may hold values from -6 to 6
- up_weight_t: bfloat16 [8256, 4096], P('tensor'), may hold values from -0.09375 to 0.09375
- up_bias: bfloat16 [8256], P('tensor'), may hold values from -4 to 4
- down_weight: bfloat16 [8256, 4096], P('tensor'), may hold values from -0.0625 to 0.0625
- kept_count: int32 [768], P(('dp', 'tensor')), may hold values from 8 to 24, as said below
Outputs:
- grad_kept: bfloat16 [18432, 4096], P(('dp', 'tensor'))
Inputs may be any that keep to these rules, and one draw needn't show every extreme that they name: `kept_count`: every block keeps at least 8 and at most 24 of its 24 slots, some block exactly 24. Among the 32 blocks of one tensor index taken in order of g, the blocks before block g keep g * 16 + e tokens together with e between -4 and 4, and e is 0 for g = 0 and for g = 32 (all 32 blocks together keep exactly 512 tokens).
All inputs are finite; a program needn't handle non-finite values.
Results may differ from a plain program's by a relative error of at most 0.014.
Values may be sent and summed in bfloat16 or wider, within the bound.
No kernel may reach another device: no remote copies, remote signals or barrier semaphores. Data moves between devices by JAX's collectives and lax.ppermute only.
A program may use at most 64 MiB of HBM per device.

v0:
```python
import jax
import jax.numpy as jnp
from jax import lax
from jax.sharding import PartitionSpec as P

BAL = 16


INV_SQRT_TWO = 0.7071067811865476
INV_SQRT_TWO_PI = 0.3989422804014327


def prefix(shard, axis, combine, identity):
    length, index = (lax.axis_size(axis), lax.axis_index(axis))
    everything = lax.all_gather(shard, axis)
    start = jnp.broadcast_to(jnp.asarray(identity, shard.dtype), shard.shape)

    def lap(k, before):
        reached = k < index
        new = combine(before, everything[k])
        return jnp.where(reached, new, before)

    return lax.fori_loop(0, length, lap, start)


def padded(block, sides, width):
    for axis, dim in sides:
        count = lax.axis_size(axis)
        forward = [(i, i + 1) for i in range(count - 1)]
        backward = [(target, source) for source, target in forward]
        low = lax.ppermute(
            lax.slice_in_dim(block, block.shape[dim] - width, None, axis=dim), axis, forward
        )
        high = lax.ppermute(lax.slice_in_dim(block, 0, width, axis=dim), axis, backward)
        block = jnp.concatenate([low, block, high], axis=dim)
    return block


def gelu_slope(values):
    return (
        0.5 * (1.0 + lax.erf(values * INV_SQRT_TWO))
        + values * jnp.exp(-0.5 * values * values) * INV_SQRT_TWO_PI
    )


def add_counts(earlier, later):
    return earlier + later


def ffn_rows(stacked, up_weight_t, up_bias, down_weight):
    contract = (((1,), (1,)), ((), ()))
    bias_wide = up_bias.astype(jnp.float32)
    piece_rows = lax.all_gather(stacked, "tensor", axis=0, tiled=True)
    inputs = piece_rows[:, 0]
    out_grads = piece_rows[:, 1]
    preact = (
        lax.dot_general(inputs, up_weight_t, contract, preferred_element_type=jnp.float32)
        + bias_wide
    )
    down_grad = lax.dot_general(
        out_grads, down_weight, contract, preferred_element_type=jnp.float32
    )
    pre_grad = (gelu_slope(preact) * down_grad).astype(jnp.bfloat16)
    partials = jnp.dot(pre_grad, up_weight_t, preferred_element_type=jnp.float32)
    return lax.psum_scatter(
        partials.astype(jnp.bfloat16), "tensor", scatter_dimension=0, tiled=True
    )


def body(kept_input, kept_grad, up_weight_t, up_bias, down_weight, kept_count):
    kmax = kept_input.shape[0]
    count_here = kept_count[0]
    entries = jnp.arange(kmax, dtype=jnp.int32)
    usable = entries < count_here
    stacked = jnp.stack((kept_input, kept_grad), axis=1)
    stacked = jnp.where(usable[:, None, None], stacked, jnp.zeros_like(stacked))
    halo_width = BAL // 4
    spots = BAL + 2 * halo_width
    first_slot = prefix(count_here, "dp", add_counts, jnp.int32(0))
    excess = first_slot - lax.axis_index("dp") * BAL
    target = excess + entries + halo_width
    placing = (target[None, :] == jnp.arange(spots, dtype=jnp.int32)[:, None]) & usable[None, :]
    placing_mat = placing.astype(jnp.bfloat16)
    outgoing = jnp.einsum(
        "sk,kcd->scd", placing_mat, stacked, preferred_element_type=jnp.float32
    ).astype(jnp.bfloat16)
    widened = padded(outgoing, (("dp", 0),), halo_width)
    owned = outgoing[halo_width : halo_width + BAL].astype(jnp.float32)
    owned = owned.at[:halo_width].add(widened[:halo_width].astype(jnp.float32))
    owned = owned.at[BAL - halo_width :].add(
        widened[widened.shape[0] - halo_width :].astype(jnp.float32)
    )
    branch = ffn_rows(owned.astype(jnp.bfloat16), up_weight_t, up_bias, down_weight)
    returned = padded(branch, (("dp", 0),), halo_width)
    own_branch = jnp.einsum(
        "sk,sd->kd", placing_mat, returned, preferred_element_type=jnp.float32
    ).astype(jnp.bfloat16)
    summed = kept_grad.astype(jnp.float32) + own_branch.astype(jnp.float32)
    return jnp.where(usable[:, None], summed, jnp.float32(0.0)).astype(jnp.bfloat16)


def solution(mesh):
    placed = (
        P(("dp", "tensor"), None),
        P(("dp", "tensor"), None),
        P("tensor", None),
        P("tensor"),
        P("tensor", None),
        P(("dp", "tensor")),
    )
    return jax.shard_map(
        body, mesh=mesh, in_specs=placed, out_specs=P(("dp", "tensor"), None), check_vma=False
    )
```

profile of v0, /device:TPU:30, one launch (start us, length us, event | category | flops | bytes accessed | tf_op | source)
XLA Modules:
  0.0 277.2 jit_solution(12591106378297774941)
XLA Ops:
  6.5 0.0 copy-start
  6.5 0.0 all-gather.2.cloned.1.call-start
  7.4 1.3 dynamic-slice.16
  8.7 0.7 dynamic-update-slice.6
  9.4 20.1 %all-reduce = s32[32]{0:T(128)S(1)} all-reduce(s32[32]{0:T(128)S(1)} %dynamic-update-slice.6), channel_id=1, replica_groups=mesh['dp'=32,'tensor'=24] {'dp'}, use_global_device_ids=true, to_apply=%add | all-reduce | flops 32 | bytes 256
  29.5 40.4 %while.15 = (s32[]{:T(128)}, s32[]{:T(128)}, s32[]{:T(128)}, s32[32]{0:T(128)S(1)}, s32[]{:T(128)}) while((s32[]{:T(128)}, s32[]{:T(128)}, s32[]{:T(128)}, s32[32]{0:T(128)S(1)}, s32[]{:T(128)}) %tuple.38), condition=%wide.region_1.2_spmd, body=%wide.region_0.1_spmd.sunk | while | flops 5 | bytes 115 | solution.py:23
  29.5 0.6 dynamic_slice.8
  30.7 0.6 dynamic_slice.8
  32.0 0.6 dynamic_slice.8
  33.3 0.6 dynamic_slice.8
  34.5 0.6 dynamic_slice.8
  35.8 0.6 dynamic_slice.8
  37.0 0.6 dynamic_slice.8
  38.3 0.6 dynamic_slice.8
  39.6 0.6 dynamic_slice.8
  40.8 0.6 dynamic_slice.8
  42.1 0.6 dynamic_slice.8
  43.4 0.6 dynamic_slice.8
  44.6 0.6 dynamic_slice.8
  45.9 0.6 dynamic_slice.8
  47.2 0.6 dynamic_slice.8
  48.4 0.6 dynamic_slice.8
  49.7 0.6 dynamic_slice.8
  51.0 0.6 dynamic_slice.8
  52.2 0.6 dynamic_slice.8
  53.5 0.6 dynamic_slice.8
  54.7 0.6 dynamic_slice.8
  56.0 0.6 dynamic_slice.8
  57.3 0.6 dynamic_slice.8
  58.5 0.6 dynamic_slice.8
  59.8 0.6 dynamic_slice.8
  61.1 0.6 dynamic_slice.8
  62.3 0.6 dynamic_slice.8
  63.6 0.6 dynamic_slice.8
  64.9 0.6 dynamic_slice.8
  66.1 0.6 dynamic_slice.8
  67.4 0.6 dynamic_slice.8
  68.7 0.6 dynamic_slice.8
  69.9 1.3 convolution_convert_fusion.1
  71.3 0.1 fusion.50
  71.3 3.3 %collective-permute-start.1 = (bf16[4,2,4096]{2,0,1:T(4,128)(2,1)S(1)}, bf16[4,2,4096]{2,0,1:T(4,128)(2,1)S(1)}, u32[]{:S(2)}, u32[]{:S(2)}) collective-permute-start(bf16[4,2,4096]{2,0,1:T(4,128)(2,1)S(1)} %get-tuple-element.117), channel_id=1, source_target_pairs={{24,0},{48,24},{72,48},{96,72},{120,96},{144,120},{168,144},{192,1... | collective-permute-start | bytes 196616 | tf_op jit(solution)/shard_map/ppermute | solution.py:34
  74.6 5.9 %collective-permute-start = (bf16[4,2,4096]{2,0,1:T(4,128)(2,1)S(1)}, bf16[4,2,4096]{2,0,1:T(4,128)(2,1)S(1)}, u32[]{:S(2)}, u32[]{:S(2)}) collective-permute-start(bf16[4,2,4096]{2,0,1:T(4,128)(2,1)S(1)} %get-tuple-element.118), channel_id=1, source_target_pairs={{0,24},{24,48},{48,72},{72,96},{96,120},{120,144},{144,168},{168,1... | collective-permute-start | bytes 196616 | tf_op jit(solution)/shard_map/ppermute | solution.py:31
  80.5 0.1 slice_convert_fusion
  80.6 1.8 collective-permute-done
  82.4 0.1 fusion.33
  82.4 0.0 collective-permute-done.1
  82.5 0.1 fusion.32
  82.5 0.7 convert_element_type.42
  83.3 0.0 all-gather.2.cloned.1.call-update
  83.3 0.0 reduce-scatter.2.cloned.1.call-start
  83.4 0.0 copy-done.1
  83.4 70.6 %all-gather.2.cloned.1.call-done = bf16[384,2,4096]{2,0,1:T(8,128)(2,1)} async-done(((bf16[16,2,4096]{2,0,1:T(8,128)(2,1)}), bf16[384,2,4096]{2,0,1:T(8,128)(2,1)}) %all-gather.2.cloned.1.call-update) | async-done | bytes 6291472 | tf_op jit(solution)/shard_map/all_gather | solution.py:53
  154.0 0.0 copy-done
  154.0 3.6 %fusion.7 = f32[384,344]{0,1:T(8,128)S(1)} fusion(bf16[344,4096]{1,0:T(8,128)(2,1)S(1)} %copy-done, bf16[384,2,4096]{2,0,1:T(8,128)(2,1)} %all-gather.2.cloned.1.call-done, f32[344]{0:T(512)S(1)} %convert_element_type.43), kind=kOutput, calls=%fused_computation.12 | convolution fusion | flops 1082262528 | bytes 6493536 | tf_op jit(solution)/shard_map/dot_general | solution.py:57
  157.6 7.9 %convolution_convert_fusion = bf16[384,4096]{1,0:T(8,128)(2,1)} fusion(bf16[344,4096]{1,0:T(8,128)(2,1)S(1)} %copy-done, bf16[344,4096]{1,0:T(8,128)(2,1)} %param.16, bf16[384,2,4096]{2,0,1:T(8,128)(2,1)} %all-gather.2.cloned.1.call-done, f32[384,344]{0,1:T(8,128)S(1)} %fusion.7), kind=kOutput, calls=%fused_computation | convolution fusion | flops 2167154688 | bytes 12455936 | tf_op jit(solution)/shard_map/dot_general | solution.py:64
  165.6 0.0 reduce-scatter.2.cloned.1.call-update
  165.6 88.3 %reduce-scatter.2.cloned.1.call-done = bf16[16,4096]{1,0:T(8,128)(2,1)} async-done(((bf16[384,4096]{1,0:T(8,128)(2,1)}), bf16[16,4096]{1,0:T(8,128)(2,1)}) %reduce-scatter.2.cloned.1.call-update) | async-done | bytes 131088 | tf_op jit(solution)/shard_map/reduce_scatter | solution.py:65
  253.9 0.9 fusion.51
  254.8 4.6 %collective-permute-start.2 = (bf16[4,4096]{1,0:T(4,128)(2,1)S(1)}, bf16[4,4096]{1,0:T(4,128)(2,1)S(1)}, u32[]{:S(2)}, u32[]{:S(2)}) collective-permute-start(bf16[4,4096]{1,0:T(4,128)(2,1)S(1)} %get-tuple-element.119), channel_id=1, source_target_pairs={{0,24},{24,48},{48,72},{72,96},{96,120},{120,144},{144,168},{168,1... | collective-permute-start | bytes 98312 | tf_op jit(solution)/shard_map/ppermute | solution.py:31
  259.4 1.9 collective-permute-start.3
  261.3 0.0 collective-permute-done.2
  261.3 7.2 %collective-permute-done.3 = bf16[4,4096]{1,0:T(4,128)(2,1)S(1)} collective-permute-done((bf16[4,4096]{1,0:T(4,128)(2,1)S(1)}, bf16[4,4096]{1,0:T(4,128)(2,1)S(1)}, u32[]{:S(2)}, u32[]{:S(2)}) %collective-permute-start.3) | collective-permute-done | bytes 32800 | tf_op jit(solution)/shard_map/ppermute | solution.py:34
  268.5 0.0 copy-done.2
  268.5 1.8 fusion.3
  (6 shorter events, 0.0 us)
Async XLA Ops:
  6.5 147.5 %copy-start = (bf16[344,4096]{1,0:T(8,128)(2,1)S(1)}, bf16[344,4096]{1,0:T(8,128)(2,1)}, u32[]{:S(2)}) copy-start(bf16[344,4096]{1,0:T(8,128)(2,1)} %param.14) | copy-start | bytes 8454148
  6.5 76.8 %copy-start.1 = (bf16[344]{0:T(512)(128)(2,1)S(1)}, bf16[344]{0:T(512)(128)(2,1)}, u32[]{:S(2)}) copy-start(bf16[344]{0:T(512)(128)(2,1)} %param.15) | copy-start | bytes 2068
  6.5 147.5 %all-gather.2.cloned.1.call-start = ((), (), s32[]{:S(2)}) async-start(), calls=%async_computation.1 | async-start | bytes 6553600 | tf_op jit(solution)/shard_map/all_gather | solution.py:53
  71.3 11.1 %collective-permute-start.1 = (bf16[4,2,4096]{2,0,1:T(4,128)(2,1)S(1)}, bf16[4,2,4096]{2,0,1:T(4,128)(2,1)S(1)}, u32[]{:S(2)}, u32[]{:S(2)}) collective-permute-start(bf16[4,2,4096]{2,0,1:T(4,128)(2,1)S(1)} %get-tuple-element.117), channel_id=1, source_target_pairs={{24,0},{48,24},{72,48},{96,72},{120,96},{144,120},{168,144},{192,1... | collective-permute-start | bytes 196616 | tf_op jit(solution)/shard_map/ppermute | solution.py:34
  74.6 7.8 %collective-permute-start = (bf16[4,2,4096]{2,0,1:T(4,128)(2,1)S(1)}, bf16[4,2,4096]{2,0,1:T(4,128)(2,1)S(1)}, u32[]{:S(2)}, u32[]{:S(2)}) collective-permute-start(bf16[4,2,4096]{2,0,1:T(4,128)(2,1)S(1)} %get-tuple-element.118), channel_id=1, source_target_pairs={{0,24},{24,48},{48,72},{72,96},{96,120},{120,144},{144,168},{168,1... | collective-permute-start | bytes 196616 | tf_op jit(solution)/shard_map/ppermute | solution.py:31
  83.3 170.6 %reduce-scatter.2.cloned.1.call-start = ((), (), s32[]{:S(2)}) async-start(), calls=%async_computation.2 | async-start | bytes 3276800 | tf_op jit(solution)/shard_map/reduce_scatter | solution.py:65
  165.6 102.9 %copy-start.2 = (bf16[24,4096]{1,0:T(8,128)(2,1)S(1)}, bf16[24,4096]{1,0:T(8,128)(2,1)}, u32[]{:S(2)}) copy-start(bf16[24,4096]{1,0:T(8,128)(2,1)} %param.13) | copy-start | bytes 589828
  254.8 6.5 %collective-permute-start.2 = (bf16[4,4096]{1,0:T(4,128)(2,1)S(1)}, bf16[4,4096]{1,0:T(4,128)(2,1)S(1)}, u32[]{:S(2)}, u32[]{:S(2)}) collective-permute-start(bf16[4,4096]{1,0:T(4,128)(2,1)S(1)} %get-tuple-element.119), channel_id=1, source_target_pairs={{0,24},{24,48},{48,72},{72,96},{96,120},{120,144},{144,168},{168,1... | collective-permute-start | bytes 98312 | tf_op jit(solution)/shard_map/ppermute | solution.py:31
  259.4 9.1 %collective-permute-start.3 = (bf16[4,4096]{1,0:T(4,128)(2,1)S(1)}, bf16[4,4096]{1,0:T(4,128)(2,1)S(1)}, u32[]{:S(2)}, u32[]{:S(2)}) collective-permute-start(bf16[4,4096]{1,0:T(4,128)(2,1)S(1)} %get-tuple-element.120), channel_id=1, source_target_pairs={{24,0},{48,24},{72,48},{96,72},{120,96},{144,120},{168,144},{192,1... | collective-permute-start | bytes 98312 | tf_op jit(solution)/shard_map/ppermute | solution.py:34
Sparse Core Ops, SparseCore 0:
  83.4 70.5 all-gather.1
  165.7 88.1 reduce-scatter.1
where the time goes:
time: 278 us; the launch traced here: 277 us
  waiting for transfers between devices  168 us (60%)
  local copies, waits for them, and re-layouts  21.7 us (8%)
  loops' own time  21.7 us (8%)
  blocking collectives  20.1 us (7%)
  starting transfers between devices  15.7 us (6%)
  matrix products  14.7 us (5%)
  between operations  14.3 us (5%)
    reduce_scatter x1, waiting for transfers between devices, ffn_rows(): lax.psum_scatter(partials.astype(jnp.bfloat16), 'tensor', scatter_dimensi...  88.3 us
    all_gather x1, waiting for transfers between devices, ffn_rows(): piece_rows = lax.all_gather(stacked, 'tensor', axis=0, tiled=True)  70.6 us
    another operation x1, loops' own time, prefix(): return lax.fori_loop(0, length, lap, start)  21.7 us
    unnamed x1, blocking collectives  20.1 us
    dynamic_slice x32, local copies, waits for them, and re-layouts, lap(): new = combine(before, everything[k])  18.8 us
    ppermute x2, starting transfers between devices, padded(): lax.ppermute(lax.slice_in_dim(block, block.shape[dim] - width, None, axis...  10.4 us
    dot_general x1, matrix products, ffn_rows(): jnp.dot(pre_grad, up_weight_t, preferred_element_type=jnp.float32)  7.95 us
    ppermute x2, waiting for transfers between devices, padded(): lax.ppermute(lax.slice_in_dim(block, 0, width, axis=dim), axis, backward)  7.19 us
  transfers between devices with their start and end apart: 6, of which 4 were waited for; matrix products, arithmetic and copies ran while one was open for 0% of the time, Pallas kernels for 0%

commit v1 on v0

v1 whole, which is shorter than its diff:
```python
import jax
import jax.numpy as jnp
from jax import lax
from jax.sharding import PartitionSpec as P

CORES = 2

INV_SQRT_TWO = 0.7071067811865476
INV_SQRT_TWO_PI = 0.3989422804014327


def gelu_slope(values):
    return (
        0.5 * (1.0 + lax.erf(values * INV_SQRT_TWO))
        + values * jnp.exp(-0.5 * values * values) * INV_SQRT_TWO_PI
    )


def with_sibling(block, pairs):
    return jnp.concatenate([block, lax.ppermute(block, "tensor", pairs)], axis=0)


def body(kept_input, kept_grad, up_weight_t, up_bias, down_weight, kept_count):
    slots = kept_input.shape[0]
    members = lax.axis_size("tensor")
    pairs = [(i, i ^ 1) for i in range(members)]
    rings = [list(range(core, members, CORES)) for core in range(CORES)]
    contract = (((1,), (1,)), ((), ()))

    stacked = jnp.stack((kept_input, kept_grad), axis=1)
    stacked, up_weight_t, up_bias, down_weight = lax.optimization_barrier(
        (stacked, up_weight_t, up_bias, down_weight)
    )
    gathered = lax.all_gather(stacked, "tensor", axis=0, tiled=True, axis_index_groups=rings)

    up = with_sibling(up_weight_t, pairs)
    down = with_sibling(down_weight, pairs)
    bias = with_sibling(up_bias, pairs).astype(jnp.float32)

    inputs = gathered[:, 0]
    out_grads = gathered[:, 1]
    preact = lax.dot_general(inputs, up, contract, preferred_element_type=jnp.float32) + bias
    down_grad = lax.dot_general(out_grads, down, contract, preferred_element_type=jnp.float32)
    pre_grad = (gelu_slope(preact) * down_grad).astype(jnp.bfloat16)
    partials = jnp.dot(pre_grad, up, preferred_element_type=jnp.float32)
    branch = lax.psum_scatter(
        partials.astype(jnp.bfloat16),
        "tensor",
        scatter_dimension=0,
        axis_index_groups=rings,
        tiled=True,
    )
    usable = jnp.arange(slots, dtype=jnp.int32) < kept_count[0]
    summed = kept_grad.astype(jnp.float32) + branch.astype(jnp.float32)
    return jnp.where(usable[:, None], summed, jnp.float32(0.0)).astype(jnp.bfloat16)


def solution(mesh):
    placed = (
        P(("dp", "tensor"), None),
        P(("dp", "tensor"), None),
        P("tensor", None),
        P("tensor"),
        P("tensor", None),
        P(("dp", "tensor")),
    )
    return jax.shard_map(
        body, mesh=mesh, in_specs=placed, out_specs=P(("dp", "tensor"), None), check_vma=False
    )
```

time: 278 us -> 173 us (0.62)
  the two profiles are of different devices: /device:TPU:30 before, /device:TPU:4 now
where the time goes in v1:
time: 173 us
  waiting for transfers between devices  126 us (73%)
  matrix products  17.3 us (10%)
  between operations  14.1 us (8%)
  starting transfers between devices  6.3 us (4%)
  local copies, waits for them, and re-layouts  5.46 us (3%)
  other arithmetic  3.6 us (2%)
    all_gather x1, waiting for transfers between devices, body(): lax.all_gather(stacked, 'tensor', axis=0, tiled=True, axis_index_groups=r...  64 us
    reduce_scatter x1, waiting for transfers between devices, body(): lax.psum_scatter(partials.astype(jnp.bfloat16), 'tensor', scatter_dimensi...  60.3 us
    dot_general x1, matrix products, body(): partials = jnp.dot(pre_grad, up, preferred_element_type=jnp.float32)  11 us
    dot_general x1, matrix products, body(): lax.dot_general(inputs, up, contract, preferred_element_type=jnp.float32)  6.29 us
    ppermute x3, starting transfers between devices, with_sibling(): lax.ppermute(block, 'tensor', pairs)  6.25 us
    unnamed x7, local copies, waits for them, and re-layouts  3.67 us
  transfers between devices with their start and end apart: 5, of which 3 were waited for; matrix products, arithmetic and copies ran while one was open for 7% of the time, Pallas kernels for 0%

profile of v1, /device:TPU:4, one launch (start us, length us, event | category | flops | bytes accessed | tf_op | source)
XLA Modules:
  0.0 172.6 jit_solution(11522979262680331326)
XLA Ops:
  6.5 0.0 copy-start.1
  6.5 0.0 all-gather.2.cloned.1.call-start
  6.5 1.8 %pad_maximum_fusion = bf16[24,2,4096]{2,0,1:T(8,128)(2,1)} fusion(bf16[24,1,4096]{2,0,1:T(8,128)(2,1)} %bitcast.20, bf16[24,1,4096]{2,0,1:T(8,128)(2,1)} %bitcast.21), kind=kLoop, calls=%fused_computation.25 | loop fusion | flops 196608 | bytes 786432 | tf_op jit(solution)/shard_map/stack | solution.py:30
  8.4 0.0 all-gather.2.cloned.1.call-update
  8.4 0.0 reduce-scatter.2.cloned.1.call-start
  8.4 1.9 %collective-permute-start = (bf16[344,4096]{1,0:T(8,128)(2,1)}, bf16[344,4096]{1,0:T(8,128)(2,1)S(1)}, u32[]{:S(2)}, u32[]{:S(2)}) collective-permute-start(bf16[344,4096]{1,0:T(8,128)(2,1)} %param.8), channel_id=1, source_target_pairs={{0,1},{1,0},{2,3},{3,2},{4,5},{5,4},{6,7},{7,6},{8,9},{9,8},{10,11... | collective-permute-start | bytes 8454152 | tf_op jit(solution)/shard_map/ppermute | solution.py:20
  10.4 2.4 %collective-permute-start.2 = (bf16[344,4096]{1,0:T(8,128)(2,1)}, bf16[344,4096]{1,0:T(8,128)(2,1)}, u32[]{:S(2)}, u32[]{:S(2)}) collective-permute-start(bf16[344,4096]{1,0:T(8,128)(2,1)} %param.10), channel_id=1, source_target_pairs={{0,1},{1,0},{2,3},{3,2},{4,5},{5,4},{6,7},{7,6},{8,9},{9,8},{10,11... | collective-permute-start | bytes 8454152 | tf_op jit(solution)/shard_map/ppermute | solution.py:20
  12.8 1.9 %collective-permute-start.1 = (bf16[344]{0:T(512)(128)(2,1)}, bf16[344]{0:T(512)(128)(2,1)S(1)}, u32[]{:S(2)}, u32[]{:S(2)}) collective-permute-start(bf16[344]{0:T(512)(128)(2,1)} %param.9), channel_id=1, source_target_pairs={{0,1},{1,0},{2,3},{3,2},{4,5},{5,4},{6,7},{7,6},{8,9},{9,8},{10,11... | collective-permute-start | bytes 2072 | tf_op jit(solution)/shard_map/ppermute | solution.py:20
  14.7 3.7 %constant_dynamic-update-slice_fusion.1 = bf16[688,4096]{1,0:T(8,128)(2,1)} fusion(bf16[344,4096]{1,0:T(8,128)(2,1)} %param.8), kind=kLoop, calls=%fused_computation.28 | loop fusion | bytes 5636096
  18.4 1.5 collective-permute-done.1
  19.9 0.0 copy-done.1
  19.9 0.1 maximum_convert_fusion
  20.0 0.0 collective-permute-done
  20.0 1.8 %constant_dynamic-update-slice_fusion = bf16[688,4096]{1,0:T(8,128)(2,1)} fusion(bf16[688,4096]{1,0:T(8,128)(2,1)} %constant_dynamic-update-slice_fusion.1, bf16[344,4096]{1,0:T(8,128)(2,1)S(1)} %collective-permute-done), kind=kLoop, calls=%fused_computation.27 | loop fusion | bytes 5636096 | tf_op jit(solution)/shard_map/concatenate | solution.py:20
  21.8 0.0 copy-start.2
  21.8 64.0 %all-gather.2.cloned.1.call-done = bf16[288,2,4096]{2,0,1:T(8,128)(2,1)} async-done(((bf16[24,2,4096]{2,0,1:T(8,128)(2,1)}), bf16[288,2,4096]{2,0,1:T(8,128)(2,1)}) %all-gather.2.cloned.1.call-update) | async-done | bytes 4718608 | tf_op jit(solution)/shard_map/all_gather | solution.py:34
  85.8 6.3 %fusion.8 = f32[288,688]{1,0:T(8,128)} fusion(bf16[688,4096]{1,0:T(8,128)(2,1)} %constant_dynamic-update-slice_fusion, bf16[288,2,4096]{2,0,1:T(8,128)(2,1)} %all-gather.2.cloned.1.call-done, f32[688]{0:T(1024)S(1)} %maximum_convert_fusion), kind=kOutput, calls=%fused_computation.10 | convolution fusion | flops 1623393792 | bytes 8790720 | tf_op jit(solution)/shard_map/dot_general | solution.py:42
  92.1 0.0 copy-start
  92.1 0.0 collective-permute-done.2
  92.1 0.0 copy-done.2
  92.1 11.0 %convolution_convert_fusion = bf16[288,4096]{1,0:T(8,128)(2,1)} fusion(bf16[688,4096]{1,0:T(8,128)(2,1)} %constant_dynamic-update-slice_fusion, bf16[344,4096]{1,0:T(8,128)(2,1)} %collective-permute-done.2, bf16[344,4096]{1,0:T(8,128)(2,1)S(1)} %copy-done.2, bf16[288,2,4096]{2,0,1:T(8,128)(2,1)} %all-gather.2.cloned.1.call-done, f32[288,688]{1,0:T(8,128)} %fusion.8), kind=kOutput, calls=%fused_computation.4 | convolution fusion | flops 3260824576 | bytes 16875520 | tf_op jit(solution)/shard_map/dot_general | solution.py:45
  103.1 0.0 reduce-scatter.2.cloned.1.call-update
  103.7 60.3 %reduce-scatter.2.cloned.1.call-done = bf16[24,4096]{1,0:T(8,128)(2,1)} async-done(((bf16[288,4096]{1,0:T(8,128)(2,1)}), bf16[24,4096]{1,0:T(8,128)(2,1)}) %reduce-scatter.2.cloned.1.call-update) | async-done | bytes 196624 | tf_op jit(solution)/shard_map/reduce_scatter | solution.py:46
  164.1 0.0 copy-done
  164.1 1.7 select_convert_fusion
  (1 shorter events, 0.0 us)
Async XLA Ops:
  6.5 13.4 %copy-start.1 = (bf16[344]{0:T(512)(128)(2,1)S(1)}, bf16[344]{0:T(512)(128)(2,1)}, u32[]{:S(2)}) copy-start(bf16[344]{0:T(512)(128)(2,1)} %param.9) | copy-start | bytes 2068
  6.5 79.3 %all-gather.2.cloned.1.call-start = ((), (), s32[]{:S(2)}) async-start(), calls=%async_computation.1 | async-start | bytes 5111808 | tf_op jit(solution)/shard_map/all_gather | solution.py:34
  8.4 155.7 %reduce-scatter.2.cloned.1.call-start = ((), (), s32[]{:S(2)}) async-start(), calls=%async_computation.2 | async-start | bytes 2555904 | tf_op jit(solution)/shard_map/reduce_scatter | solution.py:46
  8.4 11.5 %collective-permute-start = (bf16[344,4096]{1,0:T(8,128)(2,1)}, bf16[344,4096]{1,0:T(8,128)(2,1)S(1)}, u32[]{:S(2)}, u32[]{:S(2)}) collective-permute-start(bf16[344,4096]{1,0:T(8,128)(2,1)} %param.8), channel_id=1, source_target_pairs={{0,1},{1,0},{2,3},{3,2},{4,5},{5,4},{6,7},{7,6},{8,9},{9,8},{10,11... | collective-permute-start | bytes 8454152 | tf_op jit(solution)/shard_map/ppermute | solution.py:20
  10.4 81.7 %collective-permute-start.2 = (bf16[344,4096]{1,0:T(8,128)(2,1)}, bf16[344,4096]{1,0:T(8,128)(2,1)}, u32[]{:S(2)}, u32[]{:S(2)}) collective-permute-start(bf16[344,4096]{1,0:T(8,128)(2,1)} %param.10), channel_id=1, source_target_pairs={{0,1},{1,0},{2,3},{3,2},{4,5},{5,4},{6,7},{7,6},{8,9},{9,8},{10,11... | collective-permute-start | bytes 8454152 | tf_op jit(solution)/shard_map/ppermute | solution.py:20
  12.8 7.1 %collective-permute-start.1 = (bf16[344]{0:T(512)(128)(2,1)}, bf16[344]{0:T(512)(128)(2,1)S(1)}, u32[]{:S(2)}, u32[]{:S(2)}) collective-permute-start(bf16[344]{0:T(512)(128)(2,1)} %param.9), channel_id=1, source_target_pairs={{0,1},{1,0},{2,3},{3,2},{4,5},{5,4},{6,7},{7,6},{8,9},{9,8},{10,11... | collective-permute-start | bytes 2072 | tf_op jit(solution)/shard_map/ppermute | solution.py:20
  21.8 70.3 %copy-start.2 = (bf16[344,4096]{1,0:T(8,128)(2,1)S(1)}, bf16[344,4096]{1,0:T(8,128)(2,1)}, u32[]{:S(2)}) copy-start(bf16[344,4096]{1,0:T(8,128)(2,1)} %param.10) | copy-start | bytes 8454148
  92.1 72.0 %copy-start = (bf16[24,4096]{1,0:T(8,128)(2,1)S(1)}, bf16[24,4096]{1,0:T(8,128)(2,1)}, u32[]{:S(2)}) copy-start(bf16[24,4096]{1,0:T(8,128)(2,1)} %param.7) | copy-start | bytes 589828
Sparse Core Ops, SparseCore 0:
  9.7 76.0 all-gather.1
  103.2 60.8 reduce-scatter.1
